TPU v7x, 256 devices: a whole 4x4x8 slice. The times are simulated.
256 devices in a mesh: gx: 16 (over x, y), gy: 16 (over z, core).
Axes of the slice: x: 4, y: 4, z: 8, core: 2. Of those that a mesh axis runs over, the one named last changes fastest.
Arguments:
- potential: float32 [1024, 512, 128], P('gx', 'gy'), may hold values from -6 to 6
- coefficient: float32 [1024, 512, 128], P('gx', 'gy'), may hold values from -1 to 1
- shock_switch: int32 [1024, 512, 128], P('gx', 'gy'), may hold values 0 or 1
- x_factors: float32 [2, 1024, 512, 128], P(None, 'gx', 'gy'), may hold values from 0.3 to 1, as said below
- y_factors: float32 [2, 1024, 512, 128], P(None, 'gx', 'gy'), may hold values from 0.3 to 1, as said below
- wing_lead: int32 [512], P('gy'), may hold values from 0 to 255
- wing_chord: int32 [512], P('gy'), may hold values from 256 to 512
- panel_mode: int32 [1024, 512], P('gx', 'gy'), may hold values from 0 to 1
Outputs:
- correction: float32 [1024, 512, 128], P('gx', 'gy')
- station_loads: float32 [2, 512], P(None, 'gy')
Inputs may be any that keep to these rules, and one draw needn't show every extreme that they name: `x_factors`: each ratio lies strictly between 0 and 1. `y_factors`: each ratio lies strictly between 0 and 1.
All inputs are finite; a program needn't handle non-finite values. No bound on the sum of `shock_switch` on one device may be relied on, other than what follows from the above.
Results may differ from a plain program's by a relative error of at most 0.0003.
Values sent between devices are 32-bit elements; how exact they have to be, the bound alone decides.
A program may use at most 64 MiB of HBM per device.

v0:
```python
import functools

import jax
import jax.numpy as jnp
from jax import lax
from jax.experimental import pallas as pl
from jax.experimental.pallas import tpu as pltpu
from jax.sharding import PartitionSpec as P

MODES = 2
MESH = pl.DeviceIdType.MESH
F32 = jnp.float32


def complement(ratio):
    return jnp.sqrt(1.0 - ratio * ratio)


def kernel(nx, ny, I, J, Z, *refs):
    (pot, coef, switch, xf, yf, lead, chord, mode, out, loads,
     p, cf, sw, xr, yr, xq, xs, xg, xo,
     to, tg, tc, yr0, ysc, yr1, ys1, yfw, ycb, ygb, ycc,
     face_hi, face_lo, halo_lo, halo_hi, halo_prev, halo_next, strip,
     xgs, xgr, xos, xor_, xas, xar, ygs, ygr, yos, yor, yas, yar, ls, lr, ya, yb,
     load_sem, halo_send, halo_recv, push_send, push_recv) = refs
    mx = lax.axis_index("gx")
    my = lax.axis_index("gy")
    xrow, yrow = J // nx, I // ny
    U = 8

    barrier = pltpu.get_barrier_semaphore()

    def greet_x(k, _):
        pl.semaphore_signal(barrier, inc=1, device_id=(lax.rem(mx + k, nx), my), device_id_type=MESH)
        return 0

    def greet_y(k, _):
        pl.semaphore_signal(barrier, inc=1, device_id=(mx, lax.rem(my + k, ny)), device_id_type=MESH)
        return 0

    lax.fori_loop(1, nx, greet_x, 0)
    lax.fori_loop(1, ny, greet_y, 0)

    load_p = pltpu.make_async_copy(pot, p.at[pl.ds(2 * J, I * J), :], load_sem.at[0])
    load_x = pltpu.make_async_copy(xf, xr, load_sem.at[1])
    load_c = pltpu.make_async_copy(coef, cf, load_sem.at[2])
    load_s = pltpu.make_async_copy(switch, sw, load_sem.at[3])
    load_y = pltpu.make_async_copy(yf, yr, load_sem.at[4])
    for load in (load_p, load_x, load_c, load_s, load_y):
        load.start()

    def push(src, dst, along_x, slot):
        me, n = (mx, nx) if along_x else (my, ny)

        def body(k, _):
            peer = lax.rem(me + k, n)
            pltpu.make_async_remote_copy(
                src_ref=src.at[peer],
                dst_ref=dst.at[me],
                send_sem=push_send.at[slot],
                recv_sem=push_recv.at[slot],
                device_id=(peer, my) if along_x else (mx, peer),
                device_id_type=MESH,
            ).start()
            return 0

        lax.fori_loop(1, n, body, 0)

    def arrived(dst, slot):
        part = dst.at[pl.ds(0, dst.shape[0] - 1)]
        pltpu.make_async_copy(part, part, push_recv.at[slot]).wait()

    def drained(src, slot):
        part = src.at[pl.ds(0, src.shape[0] - 1)]
        pltpu.make_async_copy(part, part, push_send.at[slot]).wait()

    def at(ref, index, rows):
        return ref[pl.ds(pl.multiple_of(index * rows, 8), rows), :]

    def put(ref, index, rows, value):
        ref[pl.ds(pl.multiple_of(index * rows, 8), rows), :] = value

    def pack(dst, member, value, rows):
        total = value.shape[0]
        strip[0:total, :] = value
        for s in range(total // rows):
            dst[s, member] = strip[s * rows:(s + 1) * rows, :]

    row = lax.broadcasted_iota(jnp.int32, (J, Z), 0)
    lane = lax.broadcasted_iota(jnp.int32, (J, Z), 1)
    row8 = lax.broadcasted_iota(jnp.int32, (8, Z), 0)

    zero_line = jnp.zeros((J, Z), F32)
    p[0:J, :] = zero_line
    p[J:2 * J, :] = zero_line
    p[(I + 2) * J:(I + 3) * J, :] = zero_line
    load_p.wait()
    face_hi[...] = p[pl.ds(2 * J + J - 1, I, stride=J), :]
    face_lo[...] = p[pl.ds(2 * J, I, stride=J), :]

    load_x.wait()

    def gain_forward(c, gain):
        for u in range(U):
            i = c * U + u
            ratio = at(xr, i, J)
            put(xq, i, J, 0.25 * complement(ratio))
            gain = ratio * gain
            put(xg, i, J, gain)
        return gain

    x_gain = lax.fori_loop(0, I // U, gain_forward, jnp.ones((J, Z), F32))

    def gain_backward(c, carry):
        gain, cross = carry
        for u in range(U):
            i = I - 1 - (c * U + u)
            ratio = at(xr, I + i, J)
            scale = complement(ratio)
            put(xs, i, J, scale)
            gain = ratio * gain
            cross = ratio * cross + scale * at(xg, i, J)
            tg[pl.ds(i, J, stride=I), :] = gain
            tc[pl.ds(i, J, stride=I), :] = cross
        return gain, cross

    x_back, x_cross = lax.fori_loop(
        0, I // U, gain_backward, (jnp.ones((J, Z), F32), jnp.zeros((J, Z), F32)))
    pack(xgs, 0, x_gain, xrow)
    pack(xgs, 1, x_back, xrow)
    pack(xgs, 2, x_cross, xrow)

    pl.semaphore_wait(barrier, nx + ny - 2)

    def neighbour(src, dst, slot, device):
        return pltpu.make_async_remote_copy(
            src_ref=src, dst_ref=dst, send_sem=halo_send.at[slot], recv_sem=halo_recv.at[slot],
            device_id=device, device_id_type=MESH)

    left, right = lax.rem(mx + nx - 1, nx), lax.rem(mx + 1, nx)
    down, up = lax.rem(my + ny - 1, ny), lax.rem(my + 1, ny)
    halos = (
        neighbour(pot.at[pl.ds((I - 2) * J, 2 * J), :], halo_prev, 0, (right, my)),
        neighbour(pot.at[pl.ds(0, J), :], halo_next, 1, (left, my)),
        neighbour(face_hi, halo_lo, 2, (mx, up)),
        neighbour(face_lo, halo_hi, 3, (mx, down)),
    )
    for halo in halos:
        halo.start()
    push(xgs, xgr, True, 0)

    load_c.wait()
    load_s.wait()

    def forcing(c, _):
        for u in range(2):
            i = c * 2 + u
            before2, before, center, after = (at(p, i + d, J) for d in range(4))
            second = jnp.where(at(sw, i, J) == 1, center - 2.0 * before + before2,
                               after - 2.0 * center + before)
            span = jnp.where(row == 0, 0.0, pltpu.roll(center, 1, 0)) + jnp.where(
                row == J - 1, 0.0, pltpu.roll(center, J - 1, 0))
            normal = jnp.where(lane == 0, 0.0, pltpu.roll(center, 1, 1)) + jnp.where(
                lane == Z - 1, 0.0, pltpu.roll(center, Z - 1, 1))
            residual = at(cf, i, J) * second + (span - 2.0 * center) + (normal - 2.0 * center)
            put(xo, i, J, at(xq, i, J) * residual)
        return 0

    lax.fori_loop(0, I // 2, forcing, 0)

    for halo in halos:
        halo.wait_recv()

    before = jnp.where(mx == 0, 0.0, halo_prev[J:2 * J, :])
    before2 = jnp.where(mx == 0, 0.0, halo_prev[0:J, :])
    after = jnp.where(mx == nx - 1, 0.0, halo_next[...])
    first = jnp.where(at(sw, 0, J) == 1, before2 - 2.0 * before, before)
    second = jnp.where(at(sw, 1, J) == 1, before, 0.0)
    last = jnp.where(at(sw, I - 1, J) == 1, 0.0, after)
    for i, term in ((0, first), (1, second), (I - 1, last)):
        put(xo, i, J, at(xo, i, J) + at(xq, i, J) * (at(cf, i, J) * term))
    low = jnp.logical_and(row8 == 0, my > 0)
    high = jnp.logical_and(row8 == 7, my < ny - 1)

    def sweep_forward(c, carry):
        head, body, tail = carry
        low8 = at(halo_lo, c, U)
        high8 = at(halo_hi, c, U)
        for u in range(U):
            base = pl.multiple_of((c * U + u) * J, 8)
            r = xr[pl.ds(base, J), :]
            f = xo[pl.ds(base, J), :]
            q0 = xq[pl.ds(base, 8), :]
            q3 = xq[pl.ds(base + J - 8, 8), :]
            head = r[0:8] * head + (f[0:8] + q0 * jnp.where(low, low8[u:u + 1], 0.0))
            body = r[8:J - 8] * body + f[8:J - 8]
            tail = r[J - 8:] * tail + (f[J - 8:] + q3 * jnp.where(high, high8[u:u + 1], 0.0))
            xo[pl.ds(base, 8), :] = head
            xo[pl.ds(base + 8, J - 16), :] = body
            xo[pl.ds(base + J - 8, 8), :] = tail
        return head, body, tail

    head, body, tail = lax.fori_loop(
        0, I // U, sweep_forward,
        (jnp.zeros((8, Z), F32), jnp.zeros((J - 16, Z), F32), jnp.zeros((8, Z), F32)))

    def sweep_backward(c, state):
        for u in range(U):
            i = I - 1 - (c * U + u)
            state = at(xr, I + i, J) * state + at(xs, i, J) * at(xo, i, J)
            to[pl.ds(i, J, stride=I), :] = state
        return state

    x_first = lax.fori_loop(0, I // U, sweep_backward, jnp.zeros((J, Z), F32))
    pack(xos, 0, jnp.concatenate([head, body, tail], axis=0), xrow)
    pack(xos, 1, x_first, xrow)
    push(xos, xor_, True, 1)

    load_y.wait()

    def span_forward(c, gain):
        for u in range(2):
            j = c * 2 + u
            ratio = yr[pl.ds(j, I, stride=J), :]
            scale = complement(ratio)
            put(yr0, j, I, ratio)
            put(tg, j, I, scale * at(tg, j, I))
            put(tc, j, I, scale * at(tc, j, I))
            put(to, j, I, scale * at(to, j, I))
            gain = ratio * gain
            put(ysc, j, I, gain)
        return gain

    y_gain = lax.fori_loop(0, J // 2, span_forward, jnp.ones((I, Z), F32))

    def span_backward(c, carry):
        gain, cross = carry
        for u in range(2):
            j = J - 1 - (c * 2 + u)
            ratio = yr[pl.ds(I * J + j, I, stride=J), :]
            scale = complement(ratio)
            put(yr1, j, I, ratio)
            put(ys1, j, I, scale)
            gain = ratio * gain
            cross = ratio * cross + scale * at(ysc, j, I)
            put(ygb, j, I, gain)
            put(ycc, j, I, cross)
        return gain, cross

    y_back, y_cross = lax.fori_loop(
        0, J // 2, span_backward, (jnp.ones((I, Z), F32), jnp.zeros((I, Z), F32)))
    pack(ygs, 0, y_gain, yrow)
    pack(ygs, 1, y_back, yrow)
    pack(ygs, 2, y_cross, yrow)
    push(ygs, ygr, False, 3)

    def chain(gains, sums, gr, sr, answers, mine, me, n, rows):
        gr[me] = gains[me]
        sr[me] = sums[me]
        state = jnp.zeros((rows, Z), F32)
        partial = []
        for k in range(n):
            answers[k, 0] = state
            partial.append(sr[k, 1] + gr[k, 2] * state)
            state = sr[k, 0] + gr[k, 0] * state
        state = jnp.zeros((rows, Z), F32)
        for k in reversed(range(n)):
            answers[k, 1] = state
            state = partial[k] + gr[k, 1] * state
        mine[me] = answers[me]

    arrived(xgr, 0)
    arrived(xor_, 1)
    chain(xgs, xos, xgr, xor_, xas, xar, mx, nx, xrow)
    push(xas, xar, True, 2)
    arrived(xar, 2)

    def across(s, state):
        for t in range(xrow):
            j = s * xrow + t
            a = xar[s, 0, t:t + 1, :]
            b = xar[s, 1, t:t + 1, :]
            source = at(to, j, I) + at(tg, j, I) * b + at(tc, j, I) * a
            state = at(yr0, j, I) * state + source
            put(yfw, j, I, state)
        return state

    y_last = lax.fori_loop(0, nx, across, jnp.zeros((I, Z), F32))

    def back(c, state):
        for u in range(2):
            j = J - 1 - (c * 2 + u)
            state = at(yr1, j, I) * state + at(ys1, j, I) * at(yfw, j, I)
            put(ycb, j, I, state)
        return state

    y_first = lax.fori_loop(0, J // 2, back, jnp.zeros((I, Z), F32))
    pack(yos, 0, y_last, yrow)
    pack(yos, 1, y_first, yrow)
    push(yos, yor, False, 4)

    sign = jnp.where(lax.broadcasted_iota(jnp.int32, (I, Z), 1) == Z // 2, 1.0, 0.0) - jnp.where(
        lax.broadcasted_iota(jnp.int32, (I, Z), 1) == Z // 2 - 1, 1.0, 0.0)
    station = lax.broadcasted_iota(jnp.int32, (I, J), 1)

    def own_jump(j, jump):
        found = jnp.sum(sign * p[pl.ds(2 * J + j, I, stride=J), :], axis=1, keepdims=True)
        return jnp.where(station == j, found, jump)

    jump = lax.fori_loop(0, J, own_jump, jnp.zeros((I, J), F32))

    stream = mx * I + lax.broadcasted_iota(jnp.int32, (I, J), 0)
    owner = jnp.transpose(mode[...])
    begin = lead[...]
    length = chord[...]
    onwing = jnp.logical_and(stream >= begin, stream < begin + length)
    weight = jnp.where(onwing, 0.5 + 2.5 * stream.astype(F32) / (I * nx), 0.0) / jnp.sqrt(
        length.astype(F32))

    arrived(ygr, 3)
    arrived(yor, 4)
    chain(ygs, yos, ygr, yor, yas, yar, my, ny, yrow)
    push(yas, yar, False, 5)
    arrived(yar, 5)
    for s in range(ny):
        ya[s * yrow:(s + 1) * yrow, :] = yar[s, 0]
        yb[s * yrow:(s + 1) * yrow, :] = yar[s, 1]

    def finish(j, jump):
        value = at(ycb, j, I) + at(ygb, j, I) * yb[...] + at(ycc, j, I) * ya[...]
        out[pl.ds(j, I, stride=J), :] = value
        found = jnp.sum(sign * value, axis=1, keepdims=True)
        return jump + jnp.where(station == j, found, 0.0)

    jump = lax.fori_loop(0, J, finish, jump)
    scaled = weight * jump
    for m in range(MODES):
        ls[m:m + 1, 0:J] = jnp.sum(jnp.where(owner == m, scaled, 0.0), axis=0, keepdims=True)

    def push_loads(k, _):
        peer = lax.rem(mx + k, nx)
        pltpu.make_async_remote_copy(
            src_ref=ls, dst_ref=lr.at[mx], send_sem=push_send.at[6], recv_sem=push_recv.at[6],
            device_id=(peer, my), device_id_type=MESH).start()
        return 0

    ls[:, J:] = jnp.zeros((MODES, Z - J), F32)
    lax.fori_loop(1, nx, push_loads, 0)
    lr[mx] = ls[...]
    arrived(lr, 6)
    total = lr[0]
    for k in range(1, nx):
        total = total + lr[k]
    loads[...] = total[:, 0:J]

    for halo in halos:
        halo.wait_send()
    for src, slot in ((xgs, 0), (xos, 1), (xas, 2), (ygs, 3), (yos, 4), (yas, 5), (lr, 6)):
        drained(src, slot)


def shards(nx, ny, potential, coefficient, shock_switch, x_factors, y_factors, wing_lead, wing_chord,
           panel_mode):
    I, J, Z = potential.shape
    cells = I * J
    xrow, yrow = J // nx, I // ny
    any_space = pl.BlockSpec(memory_space=pl.ANY)
    vmem = pl.BlockSpec(memory_space=pltpu.VMEM)
    block = pltpu.VMEM((cells, Z), F32)
    face = pltpu.VMEM((I, Z), F32)
    scratch = [
        pltpu.VMEM((cells + 3 * J, Z), F32),
        block,
        pltpu.VMEM((cells, Z), jnp.int32),
        pltpu.VMEM((2 * cells, Z), F32),
        pltpu.VMEM((2 * cells, Z), F32),
    ] + [block] * 15 + [face] * 4 + [
        pltpu.VMEM((2 * J, Z), F32),
        pltpu.VMEM((J, Z), F32),
        face,
    ]
    for n, rows in ((nx, xrow), (ny, yrow)):
        for members in (3, 2, 2):
            scratch += [pltpu.VMEM((n, members, rows, Z), F32)] * 2
    scratch += [
        pltpu.VMEM((MODES, Z), F32),
        pltpu.VMEM((nx, MODES, Z), F32),
        face,
        face,
        pltpu.SemaphoreType.DMA((5,)),
        pltpu.SemaphoreType.DMA((4,)),
        pltpu.SemaphoreType.DMA((4,)),
        pltpu.SemaphoreType.DMA((7,)),
        pltpu.SemaphoreType.DMA((7,)),
    ]
    correction, loads = pl.pallas_call(
        functools.partial(kernel, nx, ny, I, J, Z),
        out_shape=(
            jax.ShapeDtypeStruct((cells, Z), F32),
            jax.ShapeDtypeStruct((MODES, J), F32),
        ),
        in_specs=[any_space] * 5 + [vmem] * 3,
        out_specs=(vmem, vmem),
        scratch_shapes=scratch,
        compiler_params=pltpu.CompilerParams(
            collective_id=0, has_side_effects=True, vmem_limit_bytes=60 * 1024 * 1024),
        name="factored_step",
    )(
        potential.reshape(cells, Z),
        coefficient.reshape(cells, Z),
        shock_switch.reshape(cells, Z),
        x_factors.reshape(2 * cells, Z),
        y_factors.reshape(2 * cells, Z),
        wing_lead.reshape(1, J),
        wing_chord.reshape(1, J),
        panel_mode.T,
    )
    return correction.reshape(I, J, Z), loads


def solution(mesh):
    placed = (
        P("gx", "gy", None),
        P("gx", "gy", None),
        P("gx", "gy", None),
        P(None, "gx", "gy", None),
        P(None, "gx", "gy", None),
        P("gy"),
        P("gy"),
        P("gx", "gy"),
    )
    return jax.shard_map(
        functools.partial(shards, mesh.shape["gx"], mesh.shape["gy"]),
        mesh=mesh,
        in_specs=placed,
        out_specs=(P("gx", "gy", None), P(None, "gy")),
        check_vma=False,
    )
```

profile of v0, /device:TPU:1, one launch (start us, length us, event | category | flops | bytes accessed | tf_op | source)
XLA Modules:
  0.0 48.9 jit_solution(15171739920855378691)
XLA Ops:
  0.6 45.4 %factored_step.1 = (f32[2048,128]{1,0:T(8,128)}, f32[2,32]{1,0:T(2,128)}) custom-call(f32[2048,128]{1,0:T(8,128)} %bitcast.12, f32[2048,128]{1,0:T(8,128)} %bitcast.13, s32[2048,128]{1,0:T(8,128)} %bitcast.14, f32[4096,128]{1,0:T(8,128)} %bitcast.9, f32[4096,128]{1,0:T(8,128)} %bitcast.10, s32[1,32]{1,0:T(1,128)} %bitcast.16, s32[1,32]{1,0:T(1,128)} %bitcast.17, ...), custom_call_target="tpu_custom_call" | custom-call | tf_op jit(solution)/shard_map/factored_step/pallas_call | solution.py:396
  46.1 0.0 copy-start
  46.1 2.3 %copy.12 = f32[64,32,128]{2,1,0:T(8,128)} copy(f32[64,32,128]{2,1,0:T(8,128)} %bitcast.11) | data formatting | bytes 2097152
  48.3 0.0 copy-done
  48.3 0.6 %copy.13 = f32[2,32]{1,0:T(2,128)} copy(f32[2,32]{1,0:T(2,128)S(1)} %copy-done) | data formatting | bytes 512
Async XLA Ops:
  46.1 2.3 %copy-start = (f32[2,32]{1,0:T(2,128)S(1)}, f32[2,32]{1,0:T(2,128)}, u32[]{:S(2)}) copy-start(f32[2,32]{1,0:T(2,128)} %get-tuple-element.9) | copy-start | bytes 772
where the time goes:
time: 49.1 us; the launch traced here: 48.9 us
  Pallas kernels  45.4 us (92%)
  local copies, waits for them, and re-layouts  2.83 us (6%)
  between operations  0.65 us (1%)
    pallas_call x1, Pallas kernels, shards(): pl.pallas_call(functools.partial(kernel, nx, ny, I, J, Z), out_shape=(jax...  45.4 us
    unnamed x4, local copies, waits for them, and re-layouts  2.83 us

commit v1 on v0

--- a/solution.py
+++ b/solution.py
@@ -22,6 +22,7 @@
      to, tg, tc, yr0, ysc, yr1, ys1, yfw, ycb, ygb, ycc,
      face_hi, face_lo, halo_lo, halo_hi, halo_prev, halo_next, strip,
      xgs, xgr, xos, xor_, xas, xar, ygs, ygr, yos, yor, yas, yar, ls, lr, ya, yb,
+     mgs, mgr, mos, mor, wide,
      load_sem, halo_send, halo_recv, push_send, push_recv) = refs
     mx = lax.axis_index("gx")
     my = lax.axis_index("gy")
@@ -49,13 +50,13 @@
     for load in (load_p, load_x, load_c, load_s, load_y):
         load.start()
 
-    def push(src, dst, along_x, slot):
+    def push(src, dst, along_x, slot, same=False):
         me, n = (mx, nx) if along_x else (my, ny)
 
         def body(k, _):
             peer = lax.rem(me + k, n)
             pltpu.make_async_remote_copy(
-                src_ref=src.at[peer],
+                src_ref=src if same else src.at[peer],
                 dst_ref=dst.at[me],
                 send_sem=push_send.at[slot],
                 recv_sem=push_recv.at[slot],
@@ -97,6 +98,33 @@
     load_p.wait()
     face_hi[...] = p[pl.ds(2 * J + J - 1, I, stride=J), :]
     face_lo[...] = p[pl.ds(2 * J, I, stride=J), :]
+
+    pl.semaphore_wait(barrier, nx + ny - 2)
+
+    def neighbour(src, dst, slot, device):
+        return pltpu.make_async_remote_copy(
+            src_ref=src, dst_ref=dst, send_sem=halo_send.at[slot], recv_sem=halo_recv.at[slot],
+            device_id=device, device_id_type=MESH)
+
+    left, right = lax.rem(mx + nx - 1, nx), lax.rem(mx + 1, nx)
+    down, up = lax.rem(my + ny - 1, ny), lax.rem(my + 1, ny)
+    halos = (
+        neighbour(pot.at[pl.ds((I - 2) * J, 2 * J), :], halo_prev, 0, (right, my)),
+        neighbour(pot.at[pl.ds(0, J), :], halo_next, 1, (left, my)),
+        neighbour(face_hi, halo_lo, 2, (mx, up)),
+        neighbour(face_lo, halo_hi, 3, (mx, down)),
+    )
+    for halo in halos:
+        halo.start()
+
+    pair = lax.broadcasted_iota(jnp.int32, (I, Z), 1) // 2
+
+    def pick(value, j, kept):
+        return jnp.where(pair == j, pltpu.roll(value, lax.rem(2 * j + Z // 2 + 1, Z), 1), kept)
+
+    def planes(upper, lower):
+        turned = jnp.transpose(jnp.concatenate([upper, lower], axis=0))
+        return turned[Z // 2 - 1:Z // 2 + 1]
 
     load_x.wait()
 
@@ -130,23 +158,6 @@
     pack(xgs, 1, x_back, xrow)
     pack(xgs, 2, x_cross, xrow)
 
-    pl.semaphore_wait(barrier, nx + ny - 2)
-
-    def neighbour(src, dst, slot, device):
-        return pltpu.make_async_remote_copy(
-            src_ref=src, dst_ref=dst, send_sem=halo_send.at[slot], recv_sem=halo_recv.at[slot],
-            device_id=device, device_id_type=MESH)
-
-    left, right = lax.rem(mx + nx - 1, nx), lax.rem(mx + 1, nx)
-    down, up = lax.rem(my + ny - 1, ny), lax.rem(my + 1, ny)
-    halos = (
-        neighbour(pot.at[pl.ds((I - 2) * J, 2 * J), :], halo_prev, 0, (right, my)),
-        neighbour(pot.at[pl.ds(0, J), :], halo_next, 1, (left, my)),
-        neighbour(face_hi, halo_lo, 2, (mx, up)),
-        neighbour(face_lo, halo_hi, 3, (mx, down)),
-    )
-    for halo in halos:
-        halo.start()
     push(xgs, xgr, True, 0)
 
     load_c.wait()
@@ -234,7 +245,7 @@
     y_gain = lax.fori_loop(0, J // 2, span_forward, jnp.ones((I, Z), F32))
 
     def span_backward(c, carry):
-        gain, cross = carry
+        gain, cross, gains2, crosses2 = carry
         for u in range(2):
             j = J - 1 - (c * 2 + u)
             ratio = yr[pl.ds(I * J + j, I, stride=J), :]
@@ -245,14 +256,22 @@
             cross = ratio * cross + scale * at(ysc, j, I)
             put(ygb, j, I, gain)
             put(ycc, j, I, cross)
-        return gain, cross
-
-    y_back, y_cross = lax.fori_loop(
-        0, J // 2, span_backward, (jnp.ones((I, Z), F32), jnp.zeros((I, Z), F32)))
+            gains2 = pick(gain, j, gains2)
+            crosses2 = pick(cross, j, crosses2)
+        return gain, cross, gains2, crosses2
+
+    zero_face = jnp.zeros((I, Z), F32)
+    y_back, y_cross, gains2, crosses2 = lax.fori_loop(
+        0, J // 2, span_backward, (jnp.ones((I, Z), F32), zero_face, zero_face, zero_face))
+    wide[0:I, :] = gains2
+    wide[I:2 * I, :] = crosses2
     pack(ygs, 0, y_gain, yrow)
     pack(ygs, 1, y_back, yrow)
     pack(ygs, 2, y_cross, yrow)
     push(ygs, ygr, False, 3)
+    mgs[0] = planes(y_gain, y_back)
+    mgs[1] = planes(y_cross, y_cross)
+    push(mgs, mgr, False, 7, True)
 
     def chain(gains, sums, gr, sr, answers, mine, me, n, rows):
         gr[me] = gains[me]
@@ -299,43 +318,59 @@
     pack(yos, 1, y_first, yrow)
     push(yos, yor, False, 4)
 
-    sign = jnp.where(lax.broadcasted_iota(jnp.int32, (I, Z), 1) == Z // 2, 1.0, 0.0) - jnp.where(
-        lax.broadcasted_iota(jnp.int32, (I, Z), 1) == Z // 2 - 1, 1.0, 0.0)
-    station = lax.broadcasted_iota(jnp.int32, (I, J), 1)
-
-    def own_jump(j, jump):
-        found = jnp.sum(sign * p[pl.ds(2 * J + j, I, stride=J), :], axis=1, keepdims=True)
-        return jnp.where(station == j, found, jump)
-
-    jump = lax.fori_loop(0, J, own_jump, jnp.zeros((I, J), F32))
-
-    stream = mx * I + lax.broadcasted_iota(jnp.int32, (I, J), 0)
-    owner = jnp.transpose(mode[...])
-    begin = lead[...]
-    length = chord[...]
+    mos[...] = planes(y_last, y_first)
+    push(mos, mor, False, 8, True)
+
+    def own_planes(j, kept):
+        return pick(p[pl.ds(2 * J + j, I, stride=J), :] + at(ycb, j, I), j, kept)
+
+    jump = lax.fori_loop(0, J, own_planes, zero_face)
+
+    stream = mx * I + lax.broadcasted_iota(jnp.int32, (J, I), 1)
+    begin = jnp.transpose(jnp.broadcast_to(lead[...], (8, J)))[:, 0:1]
+    length = jnp.transpose(jnp.broadcast_to(chord[...], (8, J)))[:, 0:1]
     onwing = jnp.logical_and(stream >= begin, stream < begin + length)
     weight = jnp.where(onwing, 0.5 + 2.5 * stream.astype(F32) / (I * nx), 0.0) / jnp.sqrt(
         length.astype(F32))
+    weights = []
+    for m in range(MODES):
+        own = jnp.concatenate(
+            [jnp.where(mode[...] == m, weight, 0.0), jnp.zeros((J, Z - I), F32)], axis=1)
+        rows = 2 * I + m * 2 * J
+        wide[pl.ds(rows, J, stride=2), :] = -own
+        wide[pl.ds(rows + 1, J, stride=2), :] = own
+        weights.append(jnp.transpose(wide[rows:rows + 2 * J, :])[0:I])
 
     arrived(ygr, 3)
     arrived(yor, 4)
     chain(ygs, yos, ygr, yor, yas, yar, my, ny, yrow)
     push(yas, yar, False, 5)
-    arrived(yar, 5)
-    for s in range(ny):
-        ya[s * yrow:(s + 1) * yrow, :] = yar[s, 0]
-        yb[s * yrow:(s + 1) * yrow, :] = yar[s, 1]
-
-    def finish(j, jump):
-        value = at(ycb, j, I) + at(ygb, j, I) * yb[...] + at(ycc, j, I) * ya[...]
-        out[pl.ds(j, I, stride=J), :] = value
-        found = jnp.sum(sign * value, axis=1, keepdims=True)
-        return jump + jnp.where(station == j, found, 0.0)
-
-    jump = lax.fori_loop(0, J, finish, jump)
-    scaled = weight * jump
+
+    arrived(mgr, 7)
+    arrived(mor, 8)
+    mgr[my] = mgs[...]
+    mor[my] = mos[...]
+    state = jnp.zeros((2, Z), F32)
+    from_left = from_right = state
+    partial = []
+    for k in range(ny):
+        from_left = jnp.where(my == k, state, from_left)
+        partial.append(mor[k] + mgr[k, 1] * pltpu.roll(state, I, 1))
+        state = mor[k] + mgr[k, 0] * state
+    state = jnp.zeros((2, Z), F32)
+    for k in reversed(range(ny)):
+        from_right = jnp.where(my == k, state, from_right)
+        state = partial[k] + mgr[k, 0] * state
+    lanes = lax.broadcasted_iota(jnp.int32, (2, Z), 1)
+    states = jnp.concatenate(
+        [jnp.where(lanes < I, from_left, from_right), jnp.zeros((6, Z), F32)], axis=0)
+    states = jnp.transpose(states)
+    odd = lax.rem(lax.broadcasted_iota(jnp.int32, (I, Z), 1), 2) == 1
+    left_state = jnp.where(odd, states[0:I, 1:2], states[0:I, 0:1])
+    right_state = jnp.where(odd, states[I:2 * I, 1:2], states[I:2 * I, 0:1])
+    jump = jump + wide[0:I, :] * right_state + wide[I:2 * I, :] * left_state
     for m in range(MODES):
-        ls[m:m + 1, 0:J] = jnp.sum(jnp.where(owner == m, scaled, 0.0), axis=0, keepdims=True)
+        ls[m:m + 1, 0:2 * J] = jnp.sum(weights[m] * jump[:, 0:2 * J], axis=0, keepdims=True)
 
     def push_loads(k, _):
         peer = lax.rem(mx + k, nx)
@@ -344,18 +379,36 @@
             device_id=(peer, my), device_id_type=MESH).start()
         return 0
 
-    ls[:, J:] = jnp.zeros((MODES, Z - J), F32)
+    ls[:, 2 * J:] = jnp.zeros((MODES, Z - 2 * J), F32)
     lax.fori_loop(1, nx, push_loads, 0)
     lr[mx] = ls[...]
+
+    arrived(yar, 5)
+    for s in range(ny):
+        ya[s * yrow:(s + 1) * yrow, :] = yar[s, 0]
+        yb[s * yrow:(s + 1) * yrow, :] = yar[s, 1]
+    a = ya[...]
+    b = yb[...]
+
+    def finish(j, _):
+        out[pl.ds(j, I, stride=J), :] = at(ycb, j, I) + at(ygb, j, I) * b + at(ycc, j, I) * a
+        return 0
+
+    lax.fori_loop(0, J, finish, 0)
+
     arrived(lr, 6)
     total = lr[0]
     for k in range(1, nx):
         total = total + lr[k]
-    loads[...] = total[:, 0:J]
+    fold = lax.broadcasted_iota(jnp.int32, (Z, J), 0) // 2 == lax.broadcasted_iota(
+        jnp.int32, (Z, J), 1)
+    loads[...] = jnp.dot(total, fold.astype(F32), precision=lax.Precision.HIGHEST,
+                         preferred_element_type=F32)
 
     for halo in halos:
         halo.wait_send()
-    for src, slot in ((xgs, 0), (xos, 1), (xas, 2), (ygs, 3), (yos, 4), (yas, 5), (lr, 6)):
+    for src, slot in ((xgs, 0), (xos, 1), (xas, 2), (ygs, 3), (yos, 4), (yas, 5), (lr, 6), (mgr, 7),
+                      (mor, 8)):
         drained(src, slot)
 
 
@@ -387,17 +440,22 @@
         pltpu.VMEM((nx, MODES, Z), F32),
         face,
         face,
+        pltpu.VMEM((2, 2, Z), F32),
+        pltpu.VMEM((ny, 2, 2, Z), F32),
+        pltpu.VMEM((2, Z), F32),
+        pltpu.VMEM((ny, 2, Z), F32),
+        pltpu.VMEM((2 * I + 2 * J * MODES, Z), F32),
         pltpu.SemaphoreType.DMA((5,)),
         pltpu.SemaphoreType.DMA((4,)),
         pltpu.SemaphoreType.DMA((4,)),
-        pltpu.SemaphoreType.DMA((7,)),
-        pltpu.SemaphoreType.DMA((7,)),
+        pltpu.SemaphoreType.DMA((9,)),
+        pltpu.SemaphoreType.DMA((9,)),
     ]
     correction, loads = pl.pallas_call(
         functools.partial(kernel, nx, ny, I, J, Z),
         out_shape=(
-            jax.ShapeDtypeStruct((cells, Z), F32),
-            jax.ShapeDtypeStruct((MODES, J), F32),
+            pltpu.VMEM((cells, Z), F32),
+            pltpu.VMEM((MODES, J), F32),
         ),
         in_specs=[any_space] * 5 + [vmem] * 3,
         out_specs=(vmem, vmem),

time: 49.1 us -> 42.2 us (0.86)
  Pallas kernels: 45.4 us -> 39.9 us
  local copies, waits for them, and re-layouts: 2.83 us -> 1.53 us
    pallas_call x1, Pallas kernels: 45.4 us -> 39.9 us  [shards(): pl.pallas_call(functools.partial(kernel, nx, ny, I, J, Z), out_shape=(plt...]
    unnamed x4 -> x2, local copies, waits for them, and re-layouts: 2.83 us -> 1.53 us
where the time goes in v1:
time: 42.2 us; the launch traced here: 42.1 us
  Pallas kernels  39.9 us (95%)
  local copies, waits for them, and re-layouts  1.53 us (4%)
  between operations  0.64 us (2%)
    pallas_call x1, Pallas kernels, shards(): pl.pallas_call(functools.partial(kernel, nx, ny, I, J, Z), out_shape=(plt...  39.9 us
    unnamed x2, local copies, waits for them, and re-layouts  1.53 us

profile of v1, /device:TPU:1, one launch (start us, length us, event | category | flops | bytes accessed | tf_op | source)
XLA Modules:
  0.0 42.1 jit_solution(14116212358369109885)
XLA Ops:
  0.6 39.9 %factored_step.1 = (f32[2048,128]{1,0:T(8,128)S(1)}, f32[2,32]{1,0:T(2,128)S(1)}) custom-call(f32[2048,128]{1,0:T(8,128)} %bitcast.12, f32[2048,128]{1,0:T(8,128)} %bitcast.13, s32[2048,128]{1,0:T(8,128)} %bitcast.14, f32[4096,128]{1,0:T(8,128)} %bitcast.10, f32[4096,128]{1,0:T(8,128)} %bitcast.11, s32[1,32]{1,0:T(1,128)} %bitcast.16, s32[1,32]{1,0:T(1,128)} %bitcast.17, ...), custom_call_target="tpu_custom_call" | custom-call | tf_op jit(solution)/shard_map/factored_step/pallas_call | solution.py:454
  40.5 1.0 %copy.12 = f32[64,32,128]{2,1,0:T(8,128)} copy(f32[64,32,128]{2,1,0:T(8,128)S(1)} %bitcast.9) | data formatting | bytes 2097152
  41.5 0.6 %copy.13 = f32[2,32]{1,0:T(2,128)} copy(f32[2,32]{1,0:T(2,128)S(1)} %get-tuple-element.7) | data formatting | bytes 512

commit v2 on v1

--- a/solution.py
+++ b/solution.py
@@ -17,12 +17,12 @@
 
 
 def kernel(nx, ny, I, J, Z, *refs):
-    (pot, coef, switch, xf, yf, lead, chord, mode, out, loads,
+    (pot, coef, switch, xf, yf, lead_hbm, chord_hbm, mode_hbm, ycb, ygb, ycc, yar, loads,
      p, cf, sw, xr, yr, xq, xs, xg, xo,
-     to, tg, tc, yr0, ysc, yr1, ys1, yfw, ycb, ygb, ycc,
+     to, tg, tc, yr0, ysc, yr1, ys1, yfw,
      face_hi, face_lo, halo_lo, halo_hi, halo_prev, halo_next, strip,
-     xgs, xgr, xos, xor_, xas, xar, ygs, ygr, yos, yor, yas, yar, ls, lr, ya, yb,
-     mgs, mgr, mos, mor, wide,
+     xgs, xgr, xos, xor_, xas, xar, ygs, ygr, yos, yor, yas, ls, lr,
+     mgs, mgr, mos, mor, wide, lead, chord, mode,
      load_sem, halo_send, halo_recv, push_send, push_recv) = refs
     mx = lax.axis_index("gx")
     my = lax.axis_index("gy")
@@ -47,7 +47,9 @@
     load_c = pltpu.make_async_copy(coef, cf, load_sem.at[2])
     load_s = pltpu.make_async_copy(switch, sw, load_sem.at[3])
     load_y = pltpu.make_async_copy(yf, yr, load_sem.at[4])
-    for load in (load_p, load_x, load_c, load_s, load_y):
+    load_w = [pltpu.make_async_copy(src, dst, load_sem.at[slot]) for src, dst, slot in (
+        (lead_hbm, lead, 5), (chord_hbm, chord, 6), (mode_hbm, mode, 7))]
+    for load in [load_p, load_x, load_c, load_s, load_y] + load_w:
         load.start()
 
     def push(src, dst, along_x, slot, same=False):
@@ -244,6 +246,26 @@
 
     y_gain = lax.fori_loop(0, J // 2, span_forward, jnp.ones((I, Z), F32))
 
+    def chain(gains, sums, gr, sr, answers, mine, me, n, rows):
+        gr[me] = gains[me]
+        sr[me] = sums[me]
+        state = jnp.zeros((rows, Z), F32)
+        partial = []
+        for k in range(n):
+            answers[k, 0] = state
+            partial.append(sr[k, 1] + gr[k, 2] * state)
+            state = sr[k, 0] + gr[k, 0] * state
+        state = jnp.zeros((rows, Z), F32)
+        for k in reversed(range(n)):
+            answers[k, 1] = state
+            state = partial[k] + gr[k, 1] * state
+        mine[me] = answers[me]
+
+    arrived(xgr, 0)
+    arrived(xor_, 1)
+    chain(xgs, xos, xgr, xor_, xas, xar, mx, nx, xrow)
+    push(xas, xar, True, 2)
+
     def span_backward(c, carry):
         gain, cross, gains2, crosses2 = carry
         for u in range(2):
@@ -273,25 +295,6 @@
     mgs[1] = planes(y_cross, y_cross)
     push(mgs, mgr, False, 7, True)
 
-    def chain(gains, sums, gr, sr, answers, mine, me, n, rows):
-        gr[me] = gains[me]
-        sr[me] = sums[me]
-        state = jnp.zeros((rows, Z), F32)
-        partial = []
-        for k in range(n):
-            answers[k, 0] = state
-            partial.append(sr[k, 1] + gr[k, 2] * state)
-            state = sr[k, 0] + gr[k, 0] * state
-        state = jnp.zeros((rows, Z), F32)
-        for k in reversed(range(n)):
-            answers[k, 1] = state
-            state = partial[k] + gr[k, 1] * state
-        mine[me] = answers[me]
-
-    arrived(xgr, 0)
-    arrived(xor_, 1)
-    chain(xgs, xos, xgr, xor_, xas, xar, mx, nx, xrow)
-    push(xas, xar, True, 2)
     arrived(xar, 2)
 
     def across(s, state):
@@ -326,6 +329,8 @@
 
     jump = lax.fori_loop(0, J, own_planes, zero_face)
 
+    for load in load_w:
+        load.wait()
     stream = mx * I + lax.broadcasted_iota(jnp.int32, (J, I), 1)
     begin = jnp.transpose(jnp.broadcast_to(lead[...], (8, J)))[:, 0:1]
     length = jnp.transpose(jnp.broadcast_to(chord[...], (8, J)))[:, 0:1]
@@ -383,19 +388,6 @@
     lax.fori_loop(1, nx, push_loads, 0)
     lr[mx] = ls[...]
 
-    arrived(yar, 5)
-    for s in range(ny):
-        ya[s * yrow:(s + 1) * yrow, :] = yar[s, 0]
-        yb[s * yrow:(s + 1) * yrow, :] = yar[s, 1]
-    a = ya[...]
-    b = yb[...]
-
-    def finish(j, _):
-        out[pl.ds(j, I, stride=J), :] = at(ycb, j, I) + at(ygb, j, I) * b + at(ycc, j, I) * a
-        return 0
-
-    lax.fori_loop(0, J, finish, 0)
-
     arrived(lr, 6)
     total = lr[0]
     for k in range(1, nx):
@@ -405,11 +397,33 @@
     loads[...] = jnp.dot(total, fold.astype(F32), precision=lax.Precision.HIGHEST,
                          preferred_element_type=F32)
 
+    arrived(yar, 5)
     for halo in halos:
         halo.wait_send()
     for src, slot in ((xgs, 0), (xos, 1), (xas, 2), (ygs, 3), (yos, 4), (yas, 5), (lr, 6), (mgr, 7),
                       (mor, 8)):
         drained(src, slot)
+
+
+def finish(I, J, Z, own, from_right, from_left, states, sums, out, loads, ya, yb, rows, sem):
+    ny, _, yrow, _ = states.shape
+    copies = [pltpu.make_async_copy(sums, loads, sem.at[0])]
+    copies[0].start()
+    for s in range(ny):
+        ya[s * yrow:(s + 1) * yrow, :] = states[s, 0]
+        yb[s * yrow:(s + 1) * yrow, :] = states[s, 1]
+    for c in range(I // 8):
+        a = ya[8 * c:8 * c + 8, :]
+        b = yb[8 * c:8 * c + 8, :]
+        for j in range(J):
+            part = pl.ds(j * I + 8 * c, 8)
+            rows[pl.ds(8 * c * J + j, 8, stride=J), :] = (
+                own[part, :] + from_right[part, :] * b + from_left[part, :] * a)
+        cells = pl.ds(8 * c * J, 8 * J)
+        copies.append(pltpu.make_async_copy(rows.at[cells, :], out.at[cells, :], sem.at[c + 1]))
+        copies[-1].start()
+    for copy in copies:
+        copy.wait()
 
 
 def shards(nx, ny, potential, coefficient, shock_switch, x_factors, y_factors, wing_lead, wing_chord,
@@ -427,7 +441,7 @@
         pltpu.VMEM((cells, Z), jnp.int32),
         pltpu.VMEM((2 * cells, Z), F32),
         pltpu.VMEM((2 * cells, Z), F32),
-    ] + [block] * 15 + [face] * 4 + [
+    ] + [block] * 12 + [face] * 4 + [
         pltpu.VMEM((2 * J, Z), F32),
         pltpu.VMEM((J, Z), F32),
         face,
@@ -435,30 +449,35 @@
     for n, rows in ((nx, xrow), (ny, yrow)):
         for members in (3, 2, 2):
             scratch += [pltpu.VMEM((n, members, rows, Z), F32)] * 2
+    scratch.pop()
     scratch += [
         pltpu.VMEM((MODES, Z), F32),
         pltpu.VMEM((nx, MODES, Z), F32),
-        face,
-        face,
         pltpu.VMEM((2, 2, Z), F32),
         pltpu.VMEM((ny, 2, 2, Z), F32),
         pltpu.VMEM((2, Z), F32),
         pltpu.VMEM((ny, 2, Z), F32),
         pltpu.VMEM((2 * I + 2 * J * MODES, Z), F32),
-        pltpu.SemaphoreType.DMA((5,)),
+        pltpu.VMEM((1, J), jnp.int32),
+        pltpu.VMEM((1, J), jnp.int32),
+        pltpu.VMEM((J, I), jnp.int32),
+        pltpu.SemaphoreType.DMA((8,)),
         pltpu.SemaphoreType.DMA((4,)),
         pltpu.SemaphoreType.DMA((4,)),
         pltpu.SemaphoreType.DMA((9,)),
         pltpu.SemaphoreType.DMA((9,)),
     ]
-    correction, loads = pl.pallas_call(
+    own, from_right, from_left, states, sums = pl.pallas_call(
         functools.partial(kernel, nx, ny, I, J, Z),
         out_shape=(
-            pltpu.VMEM((cells, Z), F32),
+            block,
+            block,
+            block,
+            pltpu.VMEM((ny, 2, yrow, Z), F32),
             pltpu.VMEM((MODES, J), F32),
         ),
-        in_specs=[any_space] * 5 + [vmem] * 3,
-        out_specs=(vmem, vmem),
+        in_specs=[any_space] * 8,
+        out_specs=(vmem,) * 5,
         scratch_shapes=scratch,
         compiler_params=pltpu.CompilerParams(
             collective_id=0, has_side_effects=True, vmem_limit_bytes=60 * 1024 * 1024),
@@ -473,6 +492,18 @@
         wing_chord.reshape(1, J),
         panel_mode.T,
     )
+    correction, loads = pl.pallas_call(
+        functools.partial(finish, I, J, Z),
+        out_shape=(
+            jax.ShapeDtypeStruct((cells, Z), F32),
+            jax.ShapeDtypeStruct((MODES, J), F32),
+        ),
+        in_specs=[vmem] * 5,
+        out_specs=(any_space, any_space),
+        scratch_shapes=[face, face, block, pltpu.SemaphoreType.DMA((I // 8 + 1,))],
+        compiler_params=pltpu.CompilerParams(vmem_limit_bytes=4 * 1024 * 1024),
+        name="finish",
+    )(own, from_right, from_left, states, sums)
     return correction.reshape(I, J, Z), loads
 
 

time: 42.2 us -> 40 us (0.948)
  local copies, waits for them, and re-layouts: 1.53 us -> 0 us
  Pallas kernels: 39.9 us -> 39.3 us
    unnamed x2 -> x0, local copies, waits for them, and re-layouts: 1.53 us -> none
    pallas_call x1 -> x2, Pallas kernels: 39.9 us -> 39.3 us  [the longest x1 37.8 us: shards(): pl.pallas_call(functools.partial(kernel, nx, ny, I, J, Z), out_shape=(blo...]
where the time goes in v2:
time: 40 us; the launch traced here: 39.9 us
  Pallas kernels  39.3 us (98%)
  between operations  0.64 us (2%)
    pallas_call x1, Pallas kernels, shards(): pl.pallas_call(functools.partial(kernel, nx, ny, I, J, Z), out_shape=(blo...  37.8 us
    pallas_call x1, Pallas kernels, shards(): pl.pallas_call(functools.partial(finish, I, J, Z), out_shape=(jax.ShapeDt...  1.52 us

profile of v2, /device:TPU:1, one launch (start us, length us, event | category | flops | bytes accessed | tf_op | source)
XLA Modules:
  0.0 39.9 jit_solution(12089961937026815357)
XLA Ops:
  0.6 37.8 %factored_step.1 = (f32[2048,128]{1,0:T(8,128)S(1)}, f32[2048,128]{1,0:T(8,128)S(1)}, f32[2048,128]{1,0:T(8,128)S(1)}, f32[16,2,4,128]{3,2,1,0:T(4,128)S(1)}, f32[2,32]{1,0:T(2,128)S(1)}) custom-call(f32[2048,128]{1,0:T(8,128)} %bitcast.11, f32[2048,128]{1,0:T(8,128)} %bitcast.12, s32[2048,128]{1,0:T(8,128)} %bitcast.13, f32[4096,128]{1,0:T(8,128)} %bitcast.9, ...), custom_call_target="tpu_custom_call" | custom-call | tf_op jit(solution)/shard_map/factored_step/pallas_call | solution.py:470
  38.4 1.5 %finish.1 = (f32[2048,128]{1,0:T(8,128)}, f32[2,32]{1,0:T(2,128)}) custom-call(f32[2048,128]{1,0:T(8,128)S(1)} %get-tuple-element.9.own, f32[2048,128]{1,0:T(8,128)S(1)} %get-tuple-element.10.from_right, f32[2048,128]{1,0:T(8,128)S(1)} %get-tuple-element.11.from_left, f32[16,2,4,128]{3,2,1,0:T(4,128)S(1)} %get-tuple-element.12.states, ...), custom_call_target="tpu_custom_call" | custom-call | tf_op jit(solution)/shard_map/finish/pallas_call | solution.py:495

commit v3 on v2

--- a/solution.py
+++ b/solution.py
@@ -10,6 +10,25 @@
 MODES = 2
 MESH = pl.DeviceIdType.MESH
 F32 = jnp.float32
+
+
+def far_first(parts):
+    spans = [()]
+    for size in parts:
+        spans = [span + (step,) for span in spans for step in range(size)]
+
+    def hops(span):
+        return sum(min(step, size - step) for step, size in zip(span, parts))
+
+    return sorted(spans[1:], key=lambda span: (-hops(span), span))
+
+
+def moved(me, span, parts):
+    place, scale = 0, 1
+    for step, size in reversed(list(zip(span, parts))):
+        place += lax.rem(lax.rem(me // scale, size) + step, size) * scale
+        scale *= size
+    return place
 
 
 def complement(ratio):
@@ -27,20 +46,14 @@
     mx = lax.axis_index("gx")
     my = lax.axis_index("gy")
     xrow, yrow = J // nx, I // ny
+    xparts, yparts = (nx // 4, 4), (ny // 2, 2)
     U = 8
 
     barrier = pltpu.get_barrier_semaphore()
 
-    def greet_x(k, _):
-        pl.semaphore_signal(barrier, inc=1, device_id=(lax.rem(mx + k, nx), my), device_id_type=MESH)
-        return 0
-
-    def greet_y(k, _):
-        pl.semaphore_signal(barrier, inc=1, device_id=(mx, lax.rem(my + k, ny)), device_id_type=MESH)
-        return 0
-
-    lax.fori_loop(1, nx, greet_x, 0)
-    lax.fori_loop(1, ny, greet_y, 0)
+    for x_span, y_span in zip(far_first(xparts), far_first(yparts)):
+        for device in ((moved(mx, x_span, xparts), my), (mx, moved(my, y_span, yparts))):
+            pl.semaphore_signal(barrier, inc=1, device_id=device, device_id_type=MESH)
 
     load_p = pltpu.make_async_copy(pot, p.at[pl.ds(2 * J, I * J), :], load_sem.at[0])
     load_x = pltpu.make_async_copy(xf, xr, load_sem.at[1])
@@ -49,14 +62,14 @@
     load_y = pltpu.make_async_copy(yf, yr, load_sem.at[4])
     load_w = [pltpu.make_async_copy(src, dst, load_sem.at[slot]) for src, dst, slot in (
         (lead_hbm, lead, 5), (chord_hbm, chord, 6), (mode_hbm, mode, 7))]
-    for load in [load_p, load_x, load_c, load_s, load_y] + load_w:
-        load.start()
+    load_p.start()
+    load_x.start()
 
     def push(src, dst, along_x, slot, same=False):
-        me, n = (mx, nx) if along_x else (my, ny)
-
-        def body(k, _):
-            peer = lax.rem(me + k, n)
+        me, parts = (mx, xparts) if along_x else (my, yparts)
+
+        for span in far_first(parts):
+            peer = moved(me, span, parts)
             pltpu.make_async_remote_copy(
                 src_ref=src if same else src.at[peer],
                 dst_ref=dst.at[me],
@@ -65,9 +78,6 @@
                 device_id=(peer, my) if along_x else (mx, peer),
                 device_id_type=MESH,
             ).start()
-            return 0
-
-        lax.fori_loop(1, n, body, 0)
 
     def arrived(dst, slot):
         part = dst.at[pl.ds(0, dst.shape[0] - 1)]
@@ -94,13 +104,6 @@
     row8 = lax.broadcasted_iota(jnp.int32, (8, Z), 0)
 
     zero_line = jnp.zeros((J, Z), F32)
-    p[0:J, :] = zero_line
-    p[J:2 * J, :] = zero_line
-    p[(I + 2) * J:(I + 3) * J, :] = zero_line
-    load_p.wait()
-    face_hi[...] = p[pl.ds(2 * J + J - 1, I, stride=J), :]
-    face_lo[...] = p[pl.ds(2 * J, I, stride=J), :]
-
     pl.semaphore_wait(barrier, nx + ny - 2)
 
     def neighbour(src, dst, slot, device):
@@ -116,8 +119,18 @@
         neighbour(face_hi, halo_lo, 2, (mx, up)),
         neighbour(face_lo, halo_hi, 3, (mx, down)),
     )
-    for halo in halos:
+    for halo in halos[:2]:
         halo.start()
+    p[0:J, :] = zero_line
+    p[J:2 * J, :] = zero_line
+    p[(I + 2) * J:(I + 3) * J, :] = zero_line
+    load_p.wait()
+    face_hi[...] = p[pl.ds(2 * J + J - 1, I, stride=J), :]
+    face_lo[...] = p[pl.ds(2 * J, I, stride=J), :]
+    for halo in halos[2:]:
+        halo.start()
+    for load in [load_c, load_s, load_y] + load_w:
+        load.start()
 
     pair = lax.broadcasted_iota(jnp.int32, (I, Z), 1) // 2
 
@@ -166,20 +179,22 @@
     load_s.wait()
 
     def forcing(c, _):
-        for u in range(2):
-            i = c * 2 + u
-            before2, before, center, after = (at(p, i + d, J) for d in range(4))
-            second = jnp.where(at(sw, i, J) == 1, center - 2.0 * before + before2,
-                               after - 2.0 * center + before)
+        rows = [at(p, c * 4 + d, J) for d in range(7)]
+        for u in range(4):
+            i = c * 4 + u
+            before2, before, center, after = rows[u:u + 4]
+            twice = center + center
+            second = jnp.where(at(sw, i, J) == 1, (center - 2.0 * before) + before2,
+                               (after - twice) + before)
             span = jnp.where(row == 0, 0.0, pltpu.roll(center, 1, 0)) + jnp.where(
                 row == J - 1, 0.0, pltpu.roll(center, J - 1, 0))
             normal = jnp.where(lane == 0, 0.0, pltpu.roll(center, 1, 1)) + jnp.where(
                 lane == Z - 1, 0.0, pltpu.roll(center, Z - 1, 1))
-            residual = at(cf, i, J) * second + (span - 2.0 * center) + (normal - 2.0 * center)
+            residual = at(cf, i, J) * second + (span - twice) + (normal - twice)
             put(xo, i, J, at(xq, i, J) * residual)
         return 0
 
-    lax.fori_loop(0, I // 2, forcing, 0)
+    lax.fori_loop(0, I // 4, forcing, 0)
 
     for halo in halos:
         halo.wait_recv()
@@ -317,12 +332,12 @@
         return state
 
     y_first = lax.fori_loop(0, J // 2, back, jnp.zeros((I, Z), F32))
+    mos[...] = planes(y_last, y_first)
+    push(mos, mor, False, 8, True)
     pack(yos, 0, y_last, yrow)
     pack(yos, 1, y_first, yrow)
     push(yos, yor, False, 4)
 
-    mos[...] = planes(y_last, y_first)
-    push(mos, mor, False, 8, True)
 
     def own_planes(j, kept):
         return pick(p[pl.ds(2 * J + j, I, stride=J), :] + at(ycb, j, I), j, kept)
@@ -377,15 +392,8 @@
     for m in range(MODES):
         ls[m:m + 1, 0:2 * J] = jnp.sum(weights[m] * jump[:, 0:2 * J], axis=0, keepdims=True)
 
-    def push_loads(k, _):
-        peer = lax.rem(mx + k, nx)
-        pltpu.make_async_remote_copy(
-            src_ref=ls, dst_ref=lr.at[mx], send_sem=push_send.at[6], recv_sem=push_recv.at[6],
-            device_id=(peer, my), device_id_type=MESH).start()
-        return 0
-
     ls[:, 2 * J:] = jnp.zeros((MODES, Z - 2 * J), F32)
-    lax.fori_loop(1, nx, push_loads, 0)
+    push(ls, lr, True, 6, True)
     lr[mx] = ls[...]
 
     arrived(lr, 6)

time: 40 us -> 38.9 us (0.972)
  Pallas kernels: 39.3 us -> 38.2 us
    pallas_call x1, Pallas kernels: 37.8 us -> 36.7 us  [shards(): pl.pallas_call(functools.partial(kernel, nx, ny, I, J, Z), out_shape=(blo...]
where the time goes in v3:
time: 38.9 us; the launch traced here: 38.8 us
  Pallas kernels  38.2 us (98%)
  between operations  0.64 us (2%)
    pallas_call x1, Pallas kernels, shards(): pl.pallas_call(functools.partial(kernel, nx, ny, I, J, Z), out_shape=(blo...  36.7 us
    pallas_call x1, Pallas kernels, shards(): pl.pallas_call(functools.partial(finish, I, J, Z), out_shape=(jax.ShapeDt...  1.52 us

profile of v3, /device:TPU:1, one launch (start us, length us, event | category | flops | bytes accessed | tf_op | source)
XLA Modules:
  0.0 38.8 jit_solution(7234756294797614861)
XLA Ops:
  0.6 36.7 %factored_step.1 = (f32[2048,128]{1,0:T(8,128)S(1)}, f32[2048,128]{1,0:T(8,128)S(1)}, f32[2048,128]{1,0:T(8,128)S(1)}, f32[16,2,4,128]{3,2,1,0:T(4,128)S(1)}, f32[2,32]{1,0:T(2,128)S(1)}) custom-call(f32[2048,128]{1,0:T(8,128)} %bitcast.11, f32[2048,128]{1,0:T(8,128)} %bitcast.12, s32[2048,128]{1,0:T(8,128)} %bitcast.13, f32[4096,128]{1,0:T(8,128)} %bitcast.9, ...), custom_call_target="tpu_custom_call" | custom-call | tf_op jit(solution)/shard_map/factored_step/pallas_call | solution.py:478
  37.3 1.5 %finish.1 = (f32[2048,128]{1,0:T(8,128)}, f32[2,32]{1,0:T(2,128)}) custom-call(f32[2048,128]{1,0:T(8,128)S(1)} %get-tuple-element.9.own, f32[2048,128]{1,0:T(8,128)S(1)} %get-tuple-element.10.from_right, f32[2048,128]{1,0:T(8,128)S(1)} %get-tuple-element.11.from_left, f32[16,2,4,128]{3,2,1,0:T(4,128)S(1)} %get-tuple-element.12.states, ...), custom_call_target="tpu_custom_call" | custom-call | tf_op jit(solution)/shard_map/finish/pallas_call | solution.py:503

commit v4 on v3

--- a/solution.py
+++ b/solution.py
@@ -312,9 +312,10 @@
 
     arrived(xar, 2)
 
-    def across(s, state):
-        for t in range(xrow):
-            j = s * xrow + t
+    def across(c, state):
+        for u in range(4 * xrow):
+            s, t = c * 4 + u // xrow, u % xrow
+            j = c * 4 * xrow + u
             a = xar[s, 0, t:t + 1, :]
             b = xar[s, 1, t:t + 1, :]
             source = at(to, j, I) + at(tg, j, I) * b + at(tc, j, I) * a
@@ -322,21 +323,21 @@
             put(yfw, j, I, state)
         return state
 
-    y_last = lax.fori_loop(0, nx, across, jnp.zeros((I, Z), F32))
+    y_last = lax.fori_loop(0, nx // 4, across, jnp.zeros((I, Z), F32))
 
     def back(c, state):
-        for u in range(2):
-            j = J - 1 - (c * 2 + u)
+        for u in range(U):
+            j = J - 1 - (c * U + u)
             state = at(yr1, j, I) * state + at(ys1, j, I) * at(yfw, j, I)
             put(ycb, j, I, state)
         return state
 
-    y_first = lax.fori_loop(0, J // 2, back, jnp.zeros((I, Z), F32))
-    mos[...] = planes(y_last, y_first)
-    push(mos, mor, False, 8, True)
+    y_first = lax.fori_loop(0, J // U, back, jnp.zeros((I, Z), F32))
     pack(yos, 0, y_last, yrow)
     pack(yos, 1, y_first, yrow)
     push(yos, yor, False, 4)
+    mos[...] = planes(y_last, y_first)
+    push(mos, mor, False, 8, True)
 
 
     def own_planes(j, kept):

time: 38.9 us -> 38.6 us (level)
  Pallas kernels: 38.2 us -> 37.8 us
where the time goes in v4:
time: 38.6 us; the launch traced here: 38.5 us
  Pallas kernels  37.8 us (98%)
  between operations  0.64 us (2%)
    pallas_call x1, Pallas kernels, shards(): pl.pallas_call(functools.partial(kernel, nx, ny, I, J, Z), out_shape=(blo...  36.3 us
    pallas_call x1, Pallas kernels, shards(): pl.pallas_call(functools.partial(finish, I, J, Z), out_shape=(jax.ShapeDt...  1.52 us

profile of v4, /device:TPU:1, one launch (start us, length us, event | category | flops | bytes accessed | tf_op | source)
XLA Modules:
  0.0 38.5 jit_solution(4071962740994632098)
XLA Ops:
  0.6 36.3 %factored_step.1 = (f32[2048,128]{1,0:T(8,128)S(1)}, f32[2048,128]{1,0:T(8,128)S(1)}, f32[2048,128]{1,0:T(8,128)S(1)}, f32[16,2,4,128]{3,2,1,0:T(4,128)S(1)}, f32[2,32]{1,0:T(2,128)S(1)}) custom-call(f32[2048,128]{1,0:T(8,128)} %bitcast.11, f32[2048,128]{1,0:T(8,128)} %bitcast.12, s32[2048,128]{1,0:T(8,128)} %bitcast.13, f32[4096,128]{1,0:T(8,128)} %bitcast.9, ...), custom_call_target="tpu_custom_call" | custom-call | tf_op jit(solution)/shard_map/factored_step/pallas_call | solution.py:479
  37.0 1.5 %finish.1 = (f32[2048,128]{1,0:T(8,128)}, f32[2,32]{1,0:T(2,128)}) custom-call(f32[2048,128]{1,0:T(8,128)S(1)} %get-tuple-element.9.own, f32[2048,128]{1,0:T(8,128)S(1)} %get-tuple-element.10.from_right, f32[2048,128]{1,0:T(8,128)S(1)} %get-tuple-element.11.from_left, f32[16,2,4,128]{3,2,1,0:T(4,128)S(1)} %get-tuple-element.12.states, ...), custom_call_target="tpu_custom_call" | custom-call | tf_op jit(solution)/shard_map/finish/pallas_call | solution.py:504

commit v5 on v4

--- a/solution.py
+++ b/solution.py
@@ -418,10 +418,10 @@
     ny, _, yrow, _ = states.shape
     copies = [pltpu.make_async_copy(sums, loads, sem.at[0])]
     copies[0].start()
-    for s in range(ny):
-        ya[s * yrow:(s + 1) * yrow, :] = states[s, 0]
-        yb[s * yrow:(s + 1) * yrow, :] = states[s, 1]
     for c in range(I // 8):
+        for s in range(c * 8 // yrow, (c + 1) * 8 // yrow):
+            ya[s * yrow:(s + 1) * yrow, :] = states[s, 0]
+            yb[s * yrow:(s + 1) * yrow, :] = states[s, 1]
         a = ya[8 * c:8 * c + 8, :]
         b = yb[8 * c:8 * c + 8, :]
         for j in range(J):

time: 38.6 us -> 38.6 us (level)
  no operation moved by 1% of the time
where the time goes in v5:
time: 38.6 us; the launch traced here: 38.5 us
  Pallas kernels  37.8 us (98%)
  between operations  0.64 us (2%)
    pallas_call x1, Pallas kernels, shards(): pl.pallas_call(functools.partial(kernel, nx, ny, I, J, Z), out_shape=(blo...  36.3 us
    pallas_call x1, Pallas kernels, shards(): pl.pallas_call(functools.partial(finish, I, J, Z), out_shape=(jax.ShapeDt...  1.51 us

profile of v5, /device:TPU:1, one launch (start us, length us, event | category | flops | bytes accessed | tf_op | source)
XLA Modules:
  0.0 38.5 jit_solution(17845860716066264109)
XLA Ops:
  0.6 36.3 %factored_step.1 = (f32[2048,128]{1,0:T(8,128)S(1)}, f32[2048,128]{1,0:T(8,128)S(1)}, f32[2048,128]{1,0:T(8,128)S(1)}, f32[16,2,4,128]{3,2,1,0:T(4,128)S(1)}, f32[2,32]{1,0:T(2,128)S(1)}) custom-call(f32[2048,128]{1,0:T(8,128)} %bitcast.11, f32[2048,128]{1,0:T(8,128)} %bitcast.12, s32[2048,128]{1,0:T(8,128)} %bitcast.13, f32[4096,128]{1,0:T(8,128)} %bitcast.9, ...), custom_call_target="tpu_custom_call" | custom-call | tf_op jit(solution)/shard_map/factored_step/pallas_call | solution.py:479
  37.0 1.5 %finish.1 = (f32[2048,128]{1,0:T(8,128)}, f32[2,32]{1,0:T(2,128)}) custom-call(f32[2048,128]{1,0:T(8,128)S(1)} %get-tuple-element.9.own, f32[2048,128]{1,0:T(8,128)S(1)} %get-tuple-element.10.from_right, f32[2048,128]{1,0:T(8,128)S(1)} %get-tuple-element.11.from_left, f32[16,2,4,128]{3,2,1,0:T(4,128)S(1)} %get-tuple-element.12.states, ...), custom_call_target="tpu_custom_call" | custom-call | tf_op jit(solution)/shard_map/finish/pallas_call | solution.py:504
